TPU v7x, 32 devices: a whole 2x2x4 slice. The times are simulated.
32 devices in a mesh: groups: 2 (over y), tile: 16 (over z, x, core).
Axes of the slice: x: 2, y: 2, z: 4, core: 2. Of those that a mesh axis runs over, the one named last changes fastest.
Arguments:
- features: bfloat16 [192, 16, 16, 256], P(('groups', 'tile')), parts along dimension 0, may hold values from -6 to 6
- weights: bfloat16 [9, 256, 256], replicated, may hold values from -0.125 to 0.125
- grad_out: bfloat16 [192, 16, 16, 256], P(('groups', 'tile')), parts along dimension 0, may hold values from -6 to 6
- tile_pos: int32 [192], P(('groups', 'tile')), parts along dimension 0, may hold values from -1 to 7, as said below
- neighbours: int32 [192, 8], P(('groups', 'tile')), parts along dimension 0, may hold values from -1 to 15, as said below
Outputs:
- activation: bfloat16 [192, 16, 16, 256], P(('groups', 'tile')), parts along dimension 0
- weight_grad: float32 [18, 256, 256], P('groups'), parts along dimension 0
- input_grad: bfloat16 [192, 16, 16, 256], P(('groups', 'tile')), parts along dimension 0
There are 2 independent parts, one for each index of `groups`. A program takes and returns all parts, laid end to end along the dimension named above; an argument that names none is the same for every part. Nothing has to cross between parts.
Inputs may be any that keep to these rules, and one draw needn't show every extreme that they name: `tile_pos`: each device's 6 slots hold the tissue tiles of its band of 2 x 4 tiles first, in raster order, then empty slots; every device holds 2 or more tissue tiles and at least one device holds 6. A code c names slot c % 6 of the device whose index is the own index plus c // 6 - 1; codes of left and right neighbours name the own device, up and up-diagonal neighbours lie on the own or the preceding device, down and down-diagonal ones on the own or the following device. Neighbours are tissue tiles of the slide's grid and the relation is symmetric; empty slots and missing neighbours have -1.
All inputs are finite; a program needn't handle non-finite values.
Results may differ from a plain program's by a relative error of at most 0.0049.
Values may be sent and summed in bfloat16 or wider, within the bound.
No kernel may reach another device: no remote copies, remote signals or barrier semaphores. Data moves between devices by JAX's collectives and lax.ppermute only.
A program may use at most 64 MiB of HBM per device.

v0:
```python
import math
import jax
import jax.numpy as jnp
from jax import lax
from jax.sharding import PartitionSpec as P

EDGE_PICK = (1, 0, 3, 2, 1, 1, 0, 0)
ROOT_HALF = 0.7071067811865476
INV_ROOT_TAU = 0.3989422804014327


def from_behind(value, axis, steps):
    count = lax.axis_size(axis)
    initial, last = (max(0, -steps), min(count, count - steps))
    return lax.ppermute(value, axis, [(source, source + steps) for source in range(initial, last)])


def gelu_value(preact):
    return preact * (0.5 * (1.0 + lax.erf(preact * ROOT_HALF)))


def gelu_slope(preact):
    cumulative = 0.5 * (1.0 + lax.erf(preact * ROOT_HALF))
    density = jnp.exp(-0.5 * preact * preact) * INV_ROOT_TAU
    return cumulative + preact * density


def edge_rims(field_map):
    return jnp.stack(
        [field_map[:, 0], field_map[:, -1], field_map[:, :, 0], field_map[:, :, -1]], axis=1
    )


def surround(center, gathered):
    upper_row = jnp.concatenate([gathered[:, 4, -1:], gathered[:, 0], gathered[:, 5, :1]], axis=1)
    lower_row = jnp.concatenate([gathered[:, 6, -1:], gathered[:, 1], gathered[:, 7, :1]], axis=1)
    middle = jnp.concatenate(
        [gathered[:, 2][:, :, None], center, gathered[:, 3][:, :, None]], axis=2
    )
    return jnp.concatenate([upper_row[:, None], middle, lower_row[:, None]], axis=1)


def tap_matrix(extended, flipped):
    side_cells = extended.shape[1] - 2
    pieces = []
    for row_tap in range(3):
        for col_tap in range(3):
            row_start = 2 - row_tap if flipped else row_tap
            col_start = 2 - col_tap if flipped else col_tap
            pieces.append(
                extended[:, row_start : row_start + side_cells, col_start : col_start + side_cells]
            )
    stacked = jnp.concatenate(pieces, axis=-1)
    return stacked.reshape(-1, stacked.shape[-1])


def lookup(edge_table, source, linked):
    clipped = jnp.clip(jnp.where(linked, source, 0), 0, edge_table.shape[0] - 1)
    picked = jnp.take(edge_table, clipped.reshape(-1), axis=0).reshape(
        linked.shape + edge_table.shape[1:]
    )
    return jnp.where(linked[:, :, None, None], picked, jnp.zeros((), picked.dtype))


def narrow_sources(neighbours, edge_picks, tile_dev):
    anchor = neighbours // tile_dev
    own_slot = (neighbours - tile_dev) * 4 + edge_picks[None, :]
    return jnp.where(
        anchor == 1,
        own_slot,
        jnp.where(anchor == 0, 4 * tile_dev + neighbours, 3 * tile_dev + neighbours),
    )


def narrow_table(own_rims, upper_rows, lower_rows):
    tile_dev = own_rims.shape[0]
    side_cells = own_rims.shape[2]
    channels = own_rims.shape[3]
    return jnp.concatenate(
        [own_rims.reshape(4 * tile_dev, side_cells, channels), upper_rows, lower_rows], axis=0
    )


def forward_tiles(extended, grad_tiles, tissue_gate, weight_mat):
    tile_count = extended.shape[0]
    side_cells = extended.shape[1] - 2
    channels = weight_mat.shape[1]
    preact = jnp.dot(tap_matrix(extended, False), weight_mat, preferred_element_type=jnp.float32)
    preact = preact.reshape(tile_count, side_cells, side_cells, channels)
    gate_cells = tissue_gate[:, None, None, None]
    act_map = (gelu_value(preact) * gate_cells).astype(jnp.bfloat16)
    slope_map = (grad_tiles.astype(jnp.float32) * gelu_slope(preact) * gate_cells).astype(
        jnp.bfloat16
    )
    return (act_map, slope_map)


def weight_terms(ext_x, slope_map):
    return lax.dot_general(
        tap_matrix(ext_x, False),
        slope_map.reshape(-1, slope_map.shape[-1]),
        (((0,), (0,)), ((), ())),
        preferred_element_type=jnp.float32,
    )


def backward_tiles(ext_g, tissue_gate, flip_mat):
    tile_count = ext_g.shape[0]
    side_cells = ext_g.shape[1] - 2
    channels = flip_mat.shape[1]
    back_map = jnp.dot(tap_matrix(ext_g, True), flip_mat, preferred_element_type=jnp.float32)
    back_map = (
        back_map.reshape(tile_count, side_cells, side_cells, channels)
        * tissue_gate[:, None, None, None]
    )
    return back_map.astype(jnp.bfloat16)


def body(features, weights, grad_out, tile_pos, neighbours):
    tile_dev = features.shape[0]
    side_cells = features.shape[1]
    channels = features.shape[3]
    devices = lax.axis_size("tile")
    tissue = (tile_pos >= 0).astype(jnp.float32)
    weight_mat = weights.reshape(9 * channels, channels)
    flip_mat = jnp.transpose(weights, (0, 2, 1)).reshape(9 * channels, channels)
    edge_picks = jnp.array(EDGE_PICK, dtype=jnp.int32)
    linked = neighbours >= 0
    rims_x = edge_rims(features)
    from_above = from_behind(rims_x[:, 1], "tile", 1)
    from_below = from_behind(rims_x[:, 0], "tile", -1)
    table_x = narrow_table(rims_x, from_above, from_below)
    source = narrow_sources(neighbours, edge_picks, tile_dev)
    ext_x = surround(features, lookup(table_x, source, linked))
    activation, pre_grad = forward_tiles(ext_x, grad_out, tissue, weight_mat)
    rims_g = edge_rims(pre_grad)
    grad_above = from_behind(rims_g[:, 1], "tile", 1)
    grad_below = from_behind(rims_g[:, 0], "tile", -1)
    table_g = narrow_table(rims_g, grad_above, grad_below)
    ext_g = surround(pre_grad, lookup(table_g, source, linked))
    weight_part = weight_terms(ext_x, pre_grad)
    grad_scale = 1.0 / math.sqrt(tile_dev * devices * side_cells * side_cells)
    summed = lax.psum(weight_part, "tile")
    weight_grad = (summed * grad_scale).reshape(9, channels, channels)
    input_grad = backward_tiles(ext_g, tissue, flip_mat)
    return (activation, weight_grad, input_grad)


def solution(mesh):
    in_specs = (
        P(("groups", "tile"), None, None, None),
        P(),
        P(("groups", "tile"), None, None, None),
        P(("groups", "tile")),
        P(("groups", "tile"), None),
    )
    out_specs = (
        P(("groups", "tile"), None, None, None),
        P("groups", None, None),
        P(("groups", "tile"), None, None, None),
    )
    return jax.shard_map(body, mesh=mesh, in_specs=in_specs, out_specs=out_specs, check_vma=False)
```

profile of v0, /device:TPU:0, one launch (start us, length us, event | category | flops | bytes accessed | tf_op | source)
XLA Modules:
  0.0 143.3 jit_solution(6044019779046628402)
XLA Ops:
  7.2 0.0 copy-start.1
  7.2 0.0 all-reduce.2.cloned.1.call-start
  7.2 0.9 slice_bitcast_fusion.11
  8.2 1.3 collective-permute-start.1
  9.5 3.0 %collective-permute-start = (bf16[6,16,256]{2,1,0:T(8,128)(2,1)S(1)}, bf16[6,16,256]{2,1,0:T(8,128)(2,1)S(1)}, u32[]{:S(2)}, u32[]{:S(2)}) collective-permute-start(bf16[6,16,256]{2,1,0:T(8,128)(2,1)S(1)} %get-tuple-element.18), channel_id=1, source_target_pairs={{0,1},{1,2},{2,3},{3,4},{4,5},{5,6},{6,7},{7,8},{8,9},{9,10},{10,1... | collective-permute-start | bytes 147464 | tf_op jit(solution)/shard_map/ppermute | solution.py:15
  12.5 1.3 fusion.14
  13.8 0.7 select_clamp_fusion
  14.5 0.1 reshape.50
  14.6 0.7 broadcast_compare_fusion
  15.3 0.7 compare_convert_fusion
  16.0 0.1 copy.60
  16.1 0.0 copy-done.1
  16.1 1.6 %copy.89 = bf16[9,256,256]{1,2,0:T(8,128)(2,1)} copy(bf16[9,256,256]{2,1,0:T(8,128)(2,1)S(1)} %copy-done.1) | data formatting | bytes 2359296 | tf_op args[1]
  17.7 0.0 copy-start
  17.7 0.0 collective-permute-done.1
  17.7 0.0 collective-permute-done
  17.8 0.6 gather_fusion
  18.3 0.1 broadcast_select_fusion.1
  18.5 0.1 copy_select_fusion.1
  18.7 0.1 copy.70
  18.7 0.1 copy.69
  18.9 0.0 copy-done
  18.9 1.2 pad_maximum_fusion
  20.2 0.1 slice_dynamic-update-slice_fusion.11
  20.2 0.3 slice_dynamic-update-slice_fusion.10
  20.6 0.3 slice_dynamic-update-slice_fusion.9
  20.9 0.4 fusion.10
  21.2 0.1 constant_dynamic-update-slice_fusion
  21.3 0.5 fusion.9
  21.8 0.0 copy-start.3
  21.8 0.1 slice_dynamic-update-slice_fusion.8
  21.9 0.3 slice_dynamic-update-slice_fusion.7
  22.2 0.3 slice_dynamic-update-slice_fusion.6
  22.5 0.4 copy-done.3
  22.9 3.6 %fusion.6 = (bf16[6,16,16,256]{3,2,1,0:T(8,128)(2,1)S(1)}, bf16[6,16,16,256]{3,2,1,0:T(8,128)(2,1)}) fusion(bf16[6,16,16,256]{3,2,1,0:T(8,128)(2,1)S(1)} %copy-done.3, f32[6]{0:T(128)S(1)} %compare_convert_fusion, bf16[6,16,16,2304]{3,2,1,0:T(8,128)(2,1)S(1)} %slice_dynamic-update-slice_fusion.6, bf16[2304,256,1,1]{1,0,3,2:T(8,128)(2,1)S(1)} %bitcast.104), kind=kOutput, calls=%fused_computation.10 | convolution fusion | flops 1817837568 | bytes 10616856 | tf_op jit(solution)/shard_map/dot_general | solution.py:88
  26.5 3.5 %convolution_bitcast_fusion = f32[2304,256]{1,0:T(8,128)} fusion(bf16[6,16,16,2304]{3,2,1,0:T(8,128)(2,1)S(1)} %slice_dynamic-update-slice_fusion.6, bf16[6,16,16,256]{3,2,1,0:T(8,128)(2,1)S(1)} %get-tuple-element.4), kind=kOutput, calls=%fused_computation.2 | convolution fusion | flops 1811939328 | bytes 10223616 | tf_op jit(solution)/shard_map/dot_general | solution.py:99
  30.0 0.2 fusion.13
  30.2 0.0 all-reduce.2.cloned.1.call-update
  30.2 1.3 collective-permute-start.3
  31.5 5.3 %collective-permute-start.2 = (bf16[6,16,256]{2,1,0:T(8,128)(2,1)S(1)}, bf16[6,16,256]{2,1,0:T(8,128)(2,1)S(1)}, u32[]{:S(2)}, u32[]{:S(2)}) collective-permute-start(bf16[6,16,256]{2,1,0:T(8,128)(2,1)S(1)} %get-tuple-element.12), channel_id=1, source_target_pairs={{0,1},{1,2},{2,3},{3,4},{4,5},{5,6},{6,7},{7,8},{8,9},{9,10},{10,1... | collective-permute-start | bytes 147464 | tf_op jit(solution)/shard_map/ppermute | solution.py:15
  36.9 0.0 collective-permute-done.3
  36.9 0.6 collective-permute-done.2
  37.6 0.6 gather_fusion.1
  38.2 0.1 broadcast_select_fusion
  38.3 0.1 copy_select_fusion
  38.5 0.1 copy.80
  38.6 0.1 copy.79
  38.7 1.2 maximum_maximum_fusion.1
  39.9 0.3 slice_dynamic-update-slice_fusion.5
  40.2 0.3 slice_dynamic-update-slice_fusion.4
  40.5 0.1 slice_dynamic-update-slice_fusion.3
  40.6 0.5 fusion.8
  41.1 0.1 constant_dynamic-update-slice_fusion.1
  41.1 0.4 fusion.7
  41.5 0.0 copy-start.2
  41.5 0.3 slice_dynamic-update-slice_fusion.2
  41.8 0.3 slice_dynamic-update-slice_fusion.1
  42.2 0.1 slice_dynamic-update-slice_fusion
  42.2 0.5 copy-done.2
  42.8 3.0 %multiply_convert_fusion = bf16[6,16,16,256]{3,2,1,0:T(8,128)(2,1)} fusion(bf16[6,16,16,2304]{3,2,1,0:T(8,128)(2,1)S(1)} %slice_dynamic-update-slice_fusion, bf16[2304,256,1,1]{1,0,3,2:T(8,128)(2,1)S(1)} %bitcast.105, f32[6]{0:T(128)S(1)} %compare_convert_fusion), kind=kOutput, calls=%fused_computation.11 | convolution fusion | flops 1812725760 | bytes 9043992 | tf_op jit(solution)/shard_map/dot_general | solution.py:111
  45.7 87.5 %all-reduce.2.cloned.1.call-done = f32[2304,256]{1,0:T(8,128)} async-done(((f32[2304,256]{1,0:T(8,128)}), f32[2304,256]{1,0:T(8,128)}) %all-reduce.2.cloned.1.call-update) | async-done | bytes 2359312 | tf_op jit(solution)/shard_map/psum | solution.py:143
  133.2 3.3 %broadcast_multiply_fusion = f32[2304,256]{1,0:T(8,128)} fusion(f32[2304,256]{1,0:T(8,128)} %all-reduce.2.cloned.1.call-done), kind=kLoop, calls=%fused_computation.18 | loop fusion | flops 589824 | bytes 4718592 | tf_op jit(solution)/shard_map/mul | solution.py:144
  (20 shorter events, 0.4 us)
Async XLA Ops:
  7.2 9.0 %copy-start.1 = (bf16[9,256,256]{2,1,0:T(8,128)(2,1)S(1)}, bf16[9,256,256]{2,1,0:T(8,128)(2,1)}, u32[]{:S(2)}) copy-start(bf16[9,256,256]{2,1,0:T(8,128)(2,1)} %param.9) | copy-start | bytes 3538948
  7.2 126.0 %all-reduce.2.cloned.1.call-start = ((), (), s32[]{:S(2)}) async-start(), calls=%async_computation | async-start | bytes 4718592 | tf_op jit(solution)/shard_map/psum | solution.py:143
  8.2 9.6 %collective-permute-start.1 = (bf16[6,16,256]{2,1,0:T(8,128)(2,1)S(1)}, bf16[6,16,256]{2,1,0:T(8,128)(2,1)S(1)}, u32[]{:S(2)}, u32[]{:S(2)}) collective-permute-start(bf16[6,16,256]{2,1,0:T(8,128)(2,1)S(1)} %get-tuple-element.17), channel_id=1, source_target_pairs={{1,0},{2,1},{3,2},{4,3},{5,4},{6,5},{7,6},{8,7},{9,8},{10,9},{11,1... | collective-permute-start | bytes 147464 | tf_op jit(solution)/shard_map/ppermute | solution.py:15
  9.5 8.3 %collective-permute-start = (bf16[6,16,256]{2,1,0:T(8,128)(2,1)S(1)}, bf16[6,16,256]{2,1,0:T(8,128)(2,1)S(1)}, u32[]{:S(2)}, u32[]{:S(2)}) collective-permute-start(bf16[6,16,256]{2,1,0:T(8,128)(2,1)S(1)} %get-tuple-element.18), channel_id=1, source_target_pairs={{0,1},{1,2},{2,3},{3,4},{4,5},{5,6},{6,7},{7,8},{8,9},{9,10},{10,1... | collective-permute-start | bytes 147464 | tf_op jit(solution)/shard_map/ppermute | solution.py:15
  17.7 1.2 copy-start
  21.8 1.1 copy-start.3
  30.2 6.7 %collective-permute-start.3 = (bf16[6,16,256]{2,1,0:T(8,128)(2,1)S(1)}, bf16[6,16,256]{2,1,0:T(8,128)(2,1)S(1)}, u32[]{:S(2)}, u32[]{:S(2)}) collective-permute-start(bf16[6,16,256]{2,1,0:T(8,128)(2,1)S(1)} %get-tuple-element.11), channel_id=1, source_target_pairs={{1,0},{2,1},{3,2},{4,3},{5,4},{6,5},{7,6},{8,7},{9,8},{10,9},{11,1... | collective-permute-start | bytes 147464 | tf_op jit(solution)/shard_map/ppermute | solution.py:15
  31.5 6.0 %collective-permute-start.2 = (bf16[6,16,256]{2,1,0:T(8,128)(2,1)S(1)}, bf16[6,16,256]{2,1,0:T(8,128)(2,1)S(1)}, u32[]{:S(2)}, u32[]{:S(2)}) collective-permute-start(bf16[6,16,256]{2,1,0:T(8,128)(2,1)S(1)} %get-tuple-element.12), channel_id=1, source_target_pairs={{0,1},{1,2},{2,3},{3,4},{4,5},{5,6},{6,7},{7,8},{8,9},{9,10},{10,1... | collective-permute-start | bytes 147464 | tf_op jit(solution)/shard_map/ppermute | solution.py:15
  41.5 1.3 copy-start.2
Sparse Core Ops, SparseCore 0:
  30.4 102.8 all-reduce.1
where the time goes:
time: 144 us; the launch traced here: 143 us
  waiting for transfers between devices  88.1 us (61%)
  between operations  14.4 us (10%)
  starting transfers between devices  11 us (8%)
  other arithmetic  10.2 us (7%)
  matrix products  10 us (7%)
  local copies, waits for them, and re-layouts  9.6 us (7%)
    psum x1, waiting for transfers between devices, body(): summed = lax.psum(weight_part, 'tile')  87.5 us
    ppermute x4, starting transfers between devices, from_behind(): lax.ppermute(value, axis, [(source, source + steps) for source in range(i...  10.9 us
    unnamed x24, local copies, waits for them, and re-layouts  5.97 us
    dot_general x1, matrix products, forward_tiles(): jnp.dot(tap_matrix(extended, False), weight_mat, preferred_element_type=j...  3.56 us
    dot_general x1, matrix products, weight_terms(): lax.dot_general(tap_matrix(ext_x, False), slope_map.reshape(-1, slope_map...  3.52 us
    mul x1, other arithmetic, body(): weight_grad = (summed * grad_scale).reshape(9, channels, channels)  3.27 us
    dot_general x1, matrix products, backward_tiles(): jnp.dot(tap_matrix(ext_g, True), flip_mat, preferred_element_type=jnp.flo...  2.96 us
  transfers between devices with their start and end apart: 5, of which 2 were waited for; matrix products, arithmetic and copies ran while one was open for 9% of the time, Pallas kernels for 0%

commit v1 on v0

--- a/solution.py
+++ b/solution.py
@@ -140,7 +140,9 @@
     ext_g = surround(pre_grad, lookup(table_g, source, linked))
     weight_part = weight_terms(ext_x, pre_grad)
     grad_scale = 1.0 / math.sqrt(tile_dev * devices * side_cells * side_cells)
-    summed = lax.psum(weight_part, "tile")
+    summed = weight_part
+    for hop in (1, 2, 4, 8):
+        summed = summed + lax.ppermute(summed, "tile", [(dev, dev ^ hop) for dev in range(16)])
     weight_grad = (summed * grad_scale).reshape(9, channels, channels)
     input_grad = backward_tiles(ext_g, tissue, flip_mat)
     return (activation, weight_grad, input_grad)

time: 144 us -> 243 us (1.69)
  waiting for transfers between devices: 88.1 us -> 191 us
  between operations: 14.4 us -> 1.05 us
  starting transfers between devices: 11 us -> 18.2 us
    ppermute x0 -> x4, waiting for transfers between devices: none -> 191 us  [body(): lax.ppermute(summed, 'tile', [(dev, dev ^ hop) for dev in range(16)])]
    psum x1 -> x0, waiting for transfers between devices: 87.5 us -> none  [body(): summed = lax.psum(weight_part, 'tile')]
    ppermute x0 -> x4, starting transfers between devices: none -> 9.37 us  [body(): lax.ppermute(summed, 'tile', [(dev, dev ^ hop) for dev in range(16)])]
    add x0 -> x3, other arithmetic: none -> 2.57 us  [body(): summed + lax.ppermute(summed, 'tile', [(dev, dev ^ hop) for dev in range(...]
  transfers between devices with their start and end apart: 5 -> 8, of which waited for: 2 -> 5; matrix products, arithmetic and copies ran while one was open for 9% -> 6% of each run, Pallas kernels for 0% -> 0%
where the time goes in v1:
time: 243 us
  waiting for transfers between devices  191 us (79%)
  starting transfers between devices  18.2 us (7%)
  other arithmetic  12.2 us (5%)
  local copies, waits for them, and re-layouts  11.4 us (5%)
  matrix products  8.66 us (4%)
    ppermute x4, waiting for transfers between devices, body(): lax.ppermute(summed, 'tile', [(dev, dev ^ hop) for dev in range(16)])  191 us
    ppermute x4, starting transfers between devices, body(): lax.ppermute(summed, 'tile', [(dev, dev ^ hop) for dev in range(16)])  9.37 us
    ppermute x4, starting transfers between devices, from_behind(): lax.ppermute(value, axis, [(source, source + steps) for source in range(i...  8.83 us
    unnamed x24, local copies, waits for them, and re-layouts  7.04 us
  transfers between devices with their start and end apart: 8, of which 5 were waited for; matrix products, arithmetic and copies ran while one was open for 6% of the time, Pallas kernels for 0%

profile of v1, /device:TPU:0, one launch (start us, length us, event | category | flops | bytes accessed | tf_op | source)
XLA Modules:
  0.0 242.8 jit_solution(3070552431671371544)
XLA Ops:
  0.6 0.8 slice_bitcast_fusion.11
  1.5 1.3 collective-permute-start.1
  2.8 3.0 %collective-permute-start = (bf16[6,16,256]{2,1,0:T(8,128)(2,1)S(1)}, bf16[6,16,256]{2,1,0:T(8,128)(2,1)S(1)}, u32[]{:S(2)}, u32[]{:S(2)}) collective-permute-start(bf16[6,16,256]{2,1,0:T(8,128)(2,1)S(1)} %get-tuple-element.18), channel_id=1, source_target_pairs={{0,1},{1,2},{2,3},{3,4},{4,5},{5,6},{6,7},{7,8},{8,9},{9,10},{10,1... | collective-permute-start | bytes 147464 | tf_op jit(solution)/shard_map/ppermute | solution.py:15
  5.8 1.3 fusion.14
  7.1 0.7 select_clamp_fusion
  7.8 0.1 reshape.50
  7.9 0.7 broadcast_compare_fusion
  8.6 0.7 compare_convert_fusion
  9.3 0.0 copy-start
  9.4 0.1 copy.60
  9.5 0.6 gather_fusion
  10.1 0.1 broadcast_select_fusion.1
  10.2 0.1 copy_select_fusion.1
  10.4 0.1 copy.70
  10.5 0.1 copy.69
  10.7 1.2 pad_maximum_fusion
  11.9 0.1 slice_dynamic-update-slice_fusion.11
  12.0 0.3 slice_dynamic-update-slice_fusion.10
  12.3 0.3 slice_dynamic-update-slice_fusion.9
  12.6 0.4 fusion.10
  13.0 0.1 constant_dynamic-update-slice_fusion
  13.1 0.5 fusion.9
  13.6 0.0 copy-start.3
  13.6 0.1 slice_dynamic-update-slice_fusion.8
  13.7 0.3 slice_dynamic-update-slice_fusion.7
  14.0 0.3 slice_dynamic-update-slice_fusion.6
  14.3 0.5 copy-done.1
  14.8 0.2 copy-done.3
  15.0 3.6 %fusion.6 = (bf16[6,16,16,256]{3,2,1,0:T(8,128)(2,1)S(1)}, bf16[6,16,16,256]{3,2,1,0:T(8,128)(2,1)}) fusion(bf16[6,16,16,256]{3,2,1,0:T(8,128)(2,1)S(1)} %copy-done.3, f32[6]{0:T(128)S(1)} %compare_convert_fusion, bf16[6,16,16,2304]{3,2,1,0:T(8,128)(2,1)S(1)} %slice_dynamic-update-slice_fusion.6, bf16[2304,256,1,1]{1,0,3,2:T(8,128)(2,1)S(1)} %bitcast.104), kind=kOutput, calls=%fused_computation.11 | convolution fusion | flops 1817837568 | bytes 10616856 | tf_op jit(solution)/shard_map/dot_general | solution.py:88
  18.6 2.1 convolution_bitcast_fusion
  20.8 2.6 %collective-permute-start.2 = (f32[2304,256]{1,0:T(8,128)S(1)}, f32[2304,256]{1,0:T(8,128)S(1)}, u32[]{:S(2)}, u32[]{:S(2)}) collective-permute-start(f32[2304,256]{1,0:T(8,128)S(1)} %convolution_bitcast_fusion), channel_id=1, source_target_pairs={{0,1},{1,0},{2,3},{3,2},{4,5},{5,4},{6,7},{7,6},{8,9},{9,8},{10,11... | collective-permute-start | bytes 7077896 | tf_op jit(solution)/shard_map/ppermute | solution.py:145
  23.4 4.2 %collective-permute-done.2 = f32[2304,256]{1,0:T(8,128)S(1)} collective-permute-done((f32[2304,256]{1,0:T(8,128)S(1)}, f32[2304,256]{1,0:T(8,128)S(1)}, u32[]{:S(2)}, u32[]{:S(2)}) %collective-permute-start.2) | collective-permute-done | bytes 2359328 | tf_op jit(solution)/shard_map/ppermute | solution.py:145
  27.6 0.3 add.55
  27.9 2.4 collective-permute-start.3
  30.3 51.8 %collective-permute-done.3 = f32[2304,256]{1,0:T(8,128)S(1)} collective-permute-done((f32[2304,256]{1,0:T(8,128)S(1)}, f32[2304,256]{1,0:T(8,128)S(1)}, u32[]{:S(2)}, u32[]{:S(2)}) %collective-permute-start.3) | collective-permute-done | bytes 2359328 | tf_op jit(solution)/shard_map/ppermute | solution.py:145
  82.1 0.3 add.56
  82.4 1.6 collective-permute-start.4
  84.0 2.4 copy.89
  86.4 1.3 collective-permute-start.7
  87.7 3.2 %collective-permute-start.6 = (bf16[6,16,256]{2,1,0:T(8,128)(2,1)S(1)}, bf16[6,16,256]{2,1,0:T(8,128)(2,1)S(1)}, u32[]{:S(2)}, u32[]{:S(2)}) collective-permute-start(bf16[6,16,256]{2,1,0:T(8,128)(2,1)S(1)} %get-tuple-element.12), channel_id=1, source_target_pairs={{0,1},{1,2},{2,3},{3,4},{4,5},{5,6},{6,7},{7,8},{8,9},{9,10},{10,1... | collective-permute-start | bytes 147464 | tf_op jit(solution)/shard_map/ppermute | solution.py:15
  90.9 0.2 fusion.13
  91.2 0.4 collective-permute-done.6
  91.7 1.3 gather_fusion.1
  93.0 1.1 broadcast_select_fusion
  94.1 0.1 copy_select_fusion
  94.3 0.1 copy.80
  94.3 0.1 copy.79
  94.5 1.2 maximum_maximum_fusion.1
  95.7 39.8 %collective-permute-done.4 = f32[2304,256]{1,0:T(8,128)} collective-permute-done((f32[2304,256]{1,0:T(8,128)S(1)}, f32[2304,256]{1,0:T(8,128)}, u32[]{:S(2)}, u32[]{:S(2)}) %collective-permute-start.4) | collective-permute-done | bytes 2359328 | tf_op jit(solution)/shard_map/ppermute | solution.py:145
  135.5 2.0 add.57
  137.5 2.7 %collective-permute-start.5 = (f32[2304,256]{1,0:T(8,128)S(1)}, f32[2304,256]{1,0:T(8,128)S(1)}, u32[]{:S(2)}, u32[]{:S(2)}) collective-permute-start(f32[2304,256]{1,0:T(8,128)S(1)} %add.57), channel_id=1, source_target_pairs={{0,8},{1,9},{2,10},{3,11},{4,12},{5,13},{6,14},{7,15},{8,0},{9,1},... | collective-permute-start | bytes 7077896 | tf_op jit(solution)/shard_map/ppermute | solution.py:145
  140.1 0.3 slice_dynamic-update-slice_fusion.5
  140.4 0.3 slice_dynamic-update-slice_fusion.4
  140.7 0.1 slice_dynamic-update-slice_fusion.3
  140.8 0.5 fusion.8
  141.3 0.1 constant_dynamic-update-slice_fusion.1
  141.4 0.4 fusion.7
  141.7 0.3 slice_dynamic-update-slice_fusion.2
  142.1 0.3 slice_dynamic-update-slice_fusion.1
  142.4 0.1 slice_dynamic-update-slice_fusion
  142.5 0.5 copy-done.2
  143.0 3.0 %multiply_convert_fusion = bf16[6,16,16,256]{3,2,1,0:T(8,128)(2,1)} fusion(bf16[6,16,16,2304]{3,2,1,0:T(8,128)(2,1)S(1)} %slice_dynamic-update-slice_fusion, bf16[2304,256,1,1]{1,0,3,2:T(8,128)(2,1)S(1)} %bitcast.105, f32[6]{0:T(128)S(1)} %compare_convert_fusion), kind=kOutput, calls=%fused_computation.12 | convolution fusion | flops 1812725760 | bytes 9043992 | tf_op jit(solution)/shard_map/dot_general | solution.py:111
  146.0 95.1 %collective-permute-done.5 = f32[2304,256]{1,0:T(8,128)S(1)} collective-permute-done((f32[2304,256]{1,0:T(8,128)S(1)}, f32[2304,256]{1,0:T(8,128)S(1)}, u32[]{:S(2)}, u32[]{:S(2)}) %collective-permute-start.5) | collective-permute-done | bytes 2359328 | tf_op jit(solution)/shard_map/ppermute | solution.py:145
  241.1 1.7 add_multiply_fusion
  (26 shorter events, 0.5 us)
Async XLA Ops:
  1.5 8.0 %collective-permute-start.1 = (bf16[6,16,256]{2,1,0:T(8,128)(2,1)S(1)}, bf16[6,16,256]{2,1,0:T(8,128)(2,1)S(1)}, u32[]{:S(2)}, u32[]{:S(2)}) collective-permute-start(bf16[6,16,256]{2,1,0:T(8,128)(2,1)S(1)} %get-tuple-element.17), channel_id=1, source_target_pairs={{1,0},{2,1},{3,2},{4,3},{5,4},{6,5},{7,6},{8,7},{9,8},{10,9},{11,1... | collective-permute-start | bytes 147464 | tf_op jit(solution)/shard_map/ppermute | solution.py:15
  2.8 6.7 %collective-permute-start = (bf16[6,16,256]{2,1,0:T(8,128)(2,1)S(1)}, bf16[6,16,256]{2,1,0:T(8,128)(2,1)S(1)}, u32[]{:S(2)}, u32[]{:S(2)}) collective-permute-start(bf16[6,16,256]{2,1,0:T(8,128)(2,1)S(1)} %get-tuple-element.18), channel_id=1, source_target_pairs={{0,1},{1,2},{2,3},{3,4},{4,5},{5,6},{6,7},{7,8},{8,9},{9,10},{10,1... | collective-permute-start | bytes 147464 | tf_op jit(solution)/shard_map/ppermute | solution.py:15
  9.3 1.4 copy-start
  13.6 1.3 copy-start.1
  13.6 1.5 copy-start.3
  20.8 6.8 %collective-permute-start.2 = (f32[2304,256]{1,0:T(8,128)S(1)}, f32[2304,256]{1,0:T(8,128)S(1)}, u32[]{:S(2)}, u32[]{:S(2)}) collective-permute-start(f32[2304,256]{1,0:T(8,128)S(1)} %convolution_bitcast_fusion), channel_id=1, source_target_pairs={{0,1},{1,0},{2,3},{3,2},{4,5},{5,4},{6,7},{7,6},{8,9},{9,8},{10,11... | collective-permute-start | bytes 7077896 | tf_op jit(solution)/shard_map/ppermute | solution.py:145
  27.9 54.2 %collective-permute-start.3 = (f32[2304,256]{1,0:T(8,128)S(1)}, f32[2304,256]{1,0:T(8,128)S(1)}, u32[]{:S(2)}, u32[]{:S(2)}) collective-permute-start(f32[2304,256]{1,0:T(8,128)S(1)} %add.55), channel_id=1, source_target_pairs={{0,2},{1,3},{2,0},{3,1},{4,6},{5,7},{6,4},{7,5},{8,10},{9,11},{10,... | collective-permute-start | bytes 7077896 | tf_op jit(solution)/shard_map/ppermute | solution.py:145
  82.4 53.1 %collective-permute-start.4 = (f32[2304,256]{1,0:T(8,128)S(1)}, f32[2304,256]{1,0:T(8,128)}, u32[]{:S(2)}, u32[]{:S(2)}) collective-permute-start(f32[2304,256]{1,0:T(8,128)S(1)} %add.56), channel_id=1, source_target_pairs={{0,4},{1,5},{2,6},{3,7},{4,0},{5,1},{6,2},{7,3},{8,12},{9,13},{10,... | collective-permute-start | bytes 7077896 | tf_op jit(solution)/shard_map/ppermute | solution.py:145
  86.4 4.8 %collective-permute-start.7 = (bf16[6,16,256]{2,1,0:T(8,128)(2,1)S(1)}, bf16[6,16,256]{2,1,0:T(8,128)(2,1)S(1)}, u32[]{:S(2)}, u32[]{:S(2)}) collective-permute-start(bf16[6,16,256]{2,1,0:T(8,128)(2,1)S(1)} %get-tuple-element.11), channel_id=1, source_target_pairs={{1,0},{2,1},{3,2},{4,3},{5,4},{6,5},{7,6},{8,7},{9,8},{10,9},{11,1... | collective-permute-start | bytes 147464 | tf_op jit(solution)/shard_map/ppermute | solution.py:15
  87.7 3.9 %collective-permute-start.6 = (bf16[6,16,256]{2,1,0:T(8,128)(2,1)S(1)}, bf16[6,16,256]{2,1,0:T(8,128)(2,1)S(1)}, u32[]{:S(2)}, u32[]{:S(2)}) collective-permute-start(bf16[6,16,256]{2,1,0:T(8,128)(2,1)S(1)} %get-tuple-element.12), channel_id=1, source_target_pairs={{0,1},{1,2},{2,3},{3,4},{4,5},{5,6},{6,7},{7,8},{8,9},{9,10},{10,1... | collective-permute-start | bytes 147464 | tf_op jit(solution)/shard_map/ppermute | solution.py:15
  137.5 103.6 %collective-permute-start.5 = (f32[2304,256]{1,0:T(8,128)S(1)}, f32[2304,256]{1,0:T(8,128)S(1)}, u32[]{:S(2)}, u32[]{:S(2)}) collective-permute-start(f32[2304,256]{1,0:T(8,128)S(1)} %add.57), channel_id=1, source_target_pairs={{0,8},{1,9},{2,10},{3,11},{4,12},{5,13},{6,14},{7,15},{8,0},{9,1},... | collective-permute-start | bytes 7077896 | tf_op jit(solution)/shard_map/ppermute | solution.py:145
  141.7 1.3 copy-start.2
